TPU v7x, 256 devices: a whole 4x4x8 slice. The times are simulated.
256 devices in a mesh: occa: 8 (over x, core), occb: 4 (over z_lo), rows: 8 (over z_hi, y).
Axes of the slice: x: 4, y: 4, z: 8 (z_hi: 2, z_lo: 4; z = z_hi * 4 + z_lo), core: 2. Of those that a mesh axis runs over, the one named last changes fastest.
Arguments:
- density: float32 [512, 8, 4, 2, 512], P('rows', 'occa', 'occb'), may hold values from -6 to 6
- operators: float32 [5, 512, 512], P(None, 'rows'), as said below
- rates: float32 [2], replicated, may hold values from 0.05 to 0.5
- coupling: float32 [2, 2], replicated, may hold values from 0.3 to 1
- keep_mask: int32 [8, 4], P('occa', 'occb'), may hold values 0 or 1
Outputs:
- advanced: float32 [512, 8, 4, 2, 512], P('rows', 'occa', 'occb')
Inputs may be any that keep to these rules, and one draw needn't show every extreme that they name: `keep_mask`: 1 keeps an auxiliary matrix in the hierarchy, 0 removes it. `operators`: each of the five matrices is symmetric.
All inputs are finite; a program needn't handle non-finite values. No bound on the sum of `keep_mask` on one device may be relied on, other than what follows from the above.
Results may differ from a plain program's by a relative error of at most 0.00005.
Values sent between devices are 32-bit elements; how exact they have to be, the bound alone decides.
A program may use at most 64 MiB of HBM per device.

v0:
```python
import jax
import jax.numpy as jnp
from jax import lax
from jax.sharding import PartitionSpec as P

TIME_STEP = 0.05
PRECISE = lax.Precision.HIGHEST


def padded(cells, sides, width):
    for axis, dim in sides:
        count = lax.axis_size(axis)
        ends = count - 1
        head = lax.slice_in_dim(cells, 0, width, axis=dim)
        tail = lax.slice_in_dim(cells, cells.shape[dim] - width, cells.shape[dim], axis=dim)
        cells = jnp.concatenate(
            [
                lax.ppermute(tail, axis, [(i, (i + 1) % count) for i in range(ends)]),
                cells,
                lax.ppermute(head, axis, [((i + 1) % count, i) for i in range(ends)]),
            ],
            axis=dim,
        )
    return cells


def neighbours(extended, count_a, count_b):
    return jnp.stack(
        [
            extended[:, 1 : count_a + 1, 1 : count_b + 1],
            extended[:, 2 : count_a + 2, 1 : count_b + 1],
            extended[:, 0:count_a, 1 : count_b + 1],
            extended[:, 1 : count_a + 1, 2 : count_b + 2],
            extended[:, 1 : count_a + 1, 0:count_b],
        ],
        axis=3,
    )


def ladder_factors(occ_a, occ_b, coupling):
    zeros = jnp.zeros_like(occ_a + occ_b)
    up_a = jnp.sqrt(occ_a + 1.0)
    up_b = jnp.sqrt(occ_b + 1.0)
    down_a = jnp.sqrt(occ_a)
    down_b = jnp.sqrt(occ_b)
    factor_re = jnp.stack(
        [zeros, zeros, down_a * coupling[0, 1], zeros, down_b * coupling[1, 1]], axis=-1
    )
    factor_im = jnp.stack(
        [zeros - 1.0, -up_a, -down_a * coupling[0, 0], -up_b, -down_b * coupling[1, 0]], axis=-1
    )
    return (factor_re, factor_im)


def weighted(stacked, factor_re, factor_im):
    part_re = stacked[..., 0, :]
    part_im = stacked[..., 1, :]
    scale_re = factor_re[None, :, :, :, None]
    scale_im = factor_im[None, :, :, :, None]
    return jnp.stack(
        [scale_re * part_re - scale_im * part_im, scale_re * part_im + scale_im * part_re], axis=4
    )


def shards(density, operators, rates, coupling, keep_mask):
    row_count = density.shape[0]
    count_a = density.shape[1]
    count_b = density.shape[2]
    full_ops = lax.all_gather(operators, "rows", axis=1, tiled=True)
    occ_a = (lax.axis_index("occa") * count_a + jnp.arange(count_a)).astype(jnp.float32)[:, None]
    occ_b = (lax.axis_index("occb") * count_b + jnp.arange(count_b)).astype(jnp.float32)[None, :]
    row_start = lax.axis_index("rows") * row_count
    factor_re, factor_im = ladder_factors(occ_a, occ_b, coupling)
    damping = (occ_a * rates[0] + occ_b * rates[1])[None, :, :, None, None]
    kept = keep_mask.astype(jnp.float32)[None, :, :, None, None]

    def derivative(field):
        extended = padded(field, (("occa", 1), ("occb", 2)), 1)
        stacked = neighbours(extended, count_a, count_b)
        right_ops = weighted(stacked, factor_re, -factor_im)
        right_part = jnp.einsum("iabkpc,kcm->iabpm", right_ops, full_ops, precision=PRECISE)
        left_ops = weighted(stacked, factor_re, factor_im)
        op_slice = lax.dynamic_slice_in_dim(full_ops, row_start, row_count, 2)
        left_part = lax.psum_scatter(
            jnp.einsum("kic,cabkpm->iabpm", op_slice, left_ops, precision=PRECISE),
            "rows",
            scatter_dimension=0,
            tiled=True,
        )
        return (left_part + right_part - damping * field) * kept

    start = density * kept
    first = derivative(start)
    second = derivative(first)
    return start + TIME_STEP * first + 0.5 * TIME_STEP * TIME_STEP * second


def solution(mesh):
    placed = (
        P("rows", "occa", "occb", None, None),
        P(None, "rows", None),
        P(),
        P(),
        P("occa", "occb"),
    )
    return jax.shard_map(
        shards,
        mesh=mesh,
        in_specs=placed,
        out_specs=P("rows", "occa", "occb", None, None),
        check_vma=False,
    )
```

profile of v0, /device:TPU:2, one launch (start us, length us, event | category | flops | bytes accessed | tf_op | source)
XLA Modules:
  0.0 391.8 jit_solution(12021623194083770563)
XLA Ops:
  6.5 0.0 all-gather.2.cloned.1.call-start
  6.5 0.7 all-gather.2.cloned.1.call-update
  7.3 0.0 copy-start.1
  7.3 0.0 reduce-scatter.3.cloned.1.call-start
  8.0 1.0 bitcast_dynamic-update-slice_fusion.5
  9.0 1.9 collective-permute-start.1
  10.9 3.6 collective-permute-start
  14.6 2.1 collective-permute-done.1
  16.7 1.8 collective-permute-done
  18.4 0.1 pad_maximum_fusion
  18.5 1.3 collective-permute-start.2
  20.0 0.0 copy-done.1
  20.0 0.7 fusion.59
  23.2 0.1 stack.103
  23.3 0.1 stack.99
  23.4 4.6 %collective-permute-start.3 = (f32[64,3,1,2,512]{4,0,3,2,1:T(8,128)S(1)}, f32[64,3,1,2,512]{4,0,3,2,1:T(8,128)S(1)}, u32[]{:S(2)}, u32[]{:S(2)}) collective-permute-start(f32[64,3,1,2,512]{4,0,3,2,1:T(8,128)S(1)} %pad_maximum_fusion), channel_id=1, source_target_pairs={{0,8},{8,16},{16,24},{1,9},{9,17},{17,25},{2,10},{10,18},{18,26},{... | collective-permute-start | bytes 2359304 | tf_op jit(solution)/shard_map/ppermute | solution.py:18
  28.0 0.1 fusion.52
  28.1 25.9 %collective-permute-done.2 = f32[64,3,1,2,512]{4,0,3,2,1:T(8,128)} collective-permute-done((f32[64,3,1,2,512]{4,0,3,2,1:T(8,128)S(1)}, f32[64,3,1,2,512]{4,0,3,2,1:T(8,128)}, u32[]{:S(2)}, u32[]{:S(2)}) %collective-permute-start.2) | collective-permute-done | bytes 786464 | tf_op jit(solution)/shard_map/ppermute | solution.py:20
  54.0 1.0 fusion.49
  54.9 2.4 collective-permute-done.3
  57.4 0.0 copy-start
  57.4 1.1 copy-done
  58.5 1.8 multiply_subtract_fusion.2
  60.3 82.9 %all-gather.2.cloned.1.call-done = f32[5,512,512]{2,1,0:T(8,128)} async-done(((f32[5,64,512]{2,1,0:T(8,128)}), f32[5,512,512]{2,1,0:T(8,128)}) %all-gather.2.cloned.1.call-update) | async-done | bytes 5242896 | tf_op jit(solution)/shard_map/all_gather | solution.py:69
  143.2 6.4 %convolution_bitcast_fusion.1 = f32[512,1,1,2,512]{4,0,3,2,1:T(8,128)} fusion(f32[64,1,1,5,1,512]{5,0,3,4,2,1:T(8,128)S(1)} %get-tuple-element.17, f32[64,1,1,5,1,512]{5,0,3,4,2,1:T(8,128)S(1)} %get-tuple-element.18, f32[5,512,512]{2,1,0:T(8,128)} %all-gather.2.cloned.1.call-done, s32[]{:T(128)S(6)} %select_n.4), kind=kOutput, calls=%fused_computation.5 | convolution fusion | flops 2013593600 | bytes 4718596 | tf_op jit(solution)/shard_map/kic,cabkpm->iabpm/dot_general | solution.py:85
  149.6 0.0 copy-start.2
  149.6 0.0 reduce-scatter.3.cloned.1.call-update
  149.6 0.0 reduce-scatter.5.cloned.1.call-start
  149.7 0.6 copy-done.2
  150.3 0.6 fusion.60
  152.1 88.1 %reduce-scatter.3.cloned.1.call-done = f32[64,1,1,2,512]{4,0,3,2,1:T(8,128)} async-done(((f32[512,1,1,2,512]{4,0,3,2,1:T(8,128)}), f32[64,1,1,2,512]{4,0,3,2,1:T(8,128)}) %reduce-scatter.3.cloned.1.call-update) | async-done | bytes 262160 | tf_op jit(solution)/shard_map/reduce_scatter | solution.py:84
  240.2 5.5 %bitcast_dynamic-update-slice_fusion.2 = (f32[64,1,1,5,2,512]{5,0,3,4,2,1:T(8,128)S(1)}, f32[64,1,1,2,512]{4,0,3,2,1:T(8,128)S(1)}) fusion(f32[]{:T(128)} %bitcast, f32[64,1,1,2,512]{4,0,3,2,1:T(8,128)S(1)} %get-tuple-element.6, f32[]{:T(128)} %bitcast.30, f32[64,1,1,2,512]{4,0,3,2,1:T(8,128)} %reduce-scatter.3.cloned.1.call-done, ...), kind=kOutput, calls=%fused_computation.54 | convolution fusion | flops 2013855744 | bytes 7602184 | tf_op jit(solution)/shard_map/iabkpc,kcm->iabpm/dot_general | solution.py:81
  245.7 1.9 collective-permute-start.5
  247.6 3.6 collective-permute-start.4
  251.3 2.1 collective-permute-done.5
  253.4 1.8 collective-permute-done.4
  255.2 0.1 pad_maximum_fusion.1
  255.2 1.3 collective-permute-start.6
  256.5 4.8 %collective-permute-start.7 = (f32[64,3,1,2,512]{4,0,3,2,1:T(8,128)S(1)}, f32[64,3,1,2,512]{4,0,3,2,1:T(8,128)S(1)}, u32[]{:S(2)}, u32[]{:S(2)}) collective-permute-start(f32[64,3,1,2,512]{4,0,3,2,1:T(8,128)S(1)} %pad_maximum_fusion.1), channel_id=1, source_target_pairs={{0,8},{8,16},{16,24},{1,9},{9,17},{17,25},{2,10},{10,18},{18,26},{... | collective-permute-start | bytes 2359304 | tf_op jit(solution)/shard_map/ppermute | solution.py:18
  261.4 15.4 %collective-permute-done.6 = f32[64,3,1,2,512]{4,0,3,2,1:T(8,128)S(1)} collective-permute-done((f32[64,3,1,2,512]{4,0,3,2,1:T(8,128)S(1)}, f32[64,3,1,2,512]{4,0,3,2,1:T(8,128)S(1)}, u32[]{:S(2)}, u32[]{:S(2)}) %collective-permute-start.6) | collective-permute-done | bytes 786464 | tf_op jit(solution)/shard_map/ppermute | solution.py:20
  276.8 1.8 collective-permute-done.7
  278.6 0.3 multiply_subtract_fusion
  278.9 6.4 %convolution_bitcast_fusion = f32[512,1,1,2,512]{4,0,3,2,1:T(8,128)} fusion(f32[64,1,1,5,1,512]{5,0,3,4,2,1:T(8,128)S(1)} %get-tuple-element.15, f32[64,1,1,5,1,512]{5,0,3,4,2,1:T(8,128)S(1)} %get-tuple-element.16, f32[5,512,512]{2,1,0:T(8,128)} %all-gather.2.cloned.1.call-done, s32[]{:T(128)S(6)} %select_n.4), kind=kOutput, calls=%fused_computation.4 | convolution fusion | flops 2013593600 | bytes 4718596 | tf_op jit(solution)/shard_map/kic,cabkpm->iabpm/dot_general | solution.py:85
  285.3 0.0 reduce-scatter.5.cloned.1.call-update
  285.3 93.4 %reduce-scatter.5.cloned.1.call-done = f32[64,1,1,2,512]{4,0,3,2,1:T(8,128)} async-done(((f32[512,1,1,2,512]{4,0,3,2,1:T(8,128)}), f32[64,1,1,2,512]{4,0,3,2,1:T(8,128)}) %reduce-scatter.5.cloned.1.call-update) | async-done | bytes 262160 | tf_op jit(solution)/shard_map/reduce_scatter | solution.py:84
  378.8 5.5 %fusion.34 = f32[64,1,1,2,512]{4,0,3,2,1:T(8,128)S(1)} fusion(f32[64,1,1,2,512]{4,0,3,2,1:T(8,128)} %reduce-scatter.5.cloned.1.call-done, f32[5,512,512]{2,1,0:T(8,128)} %all-gather.2.cloned.1.call-done, f32[64,1,1,5,1,512]{5,0,3,4,2,1:T(8,128)S(1)} %get-tuple-element.8, f32[64,1,1,5,1,512]{5,0,3,4,2,1:T(8,128)S(1)} %get-tuple-element.7, ...), kind=kOutput, calls=%fused_computation.28 | convolution fusion | flops 2014117888 | bytes 7602184 | tf_op jit(solution)/shard_map/iabkpc,kcm->iabpm/dot_general | solution.py:81
  384.3 0.9 copy.25
  (9 shorter events, 0.1 us)
Async XLA Ops:
  6.5 136.7 %all-gather.2.cloned.1.call-start = ((), (), s32[]{:S(2)}) async-start(), calls=%async_computation.2 | async-start | bytes 5898240 | tf_op jit(solution)/shard_map/all_gather | solution.py:69
  7.3 12.7 %copy-start.1 = (f32[2,2]{1,0:T(2,128)S(1)}, f32[2,2]{1,0:T(2,128)}, u32[]{:S(2)}) copy-start(f32[2,2]{1,0:T(2,128)} %param.8) | copy-start | bytes 52
  7.3 232.9 %reduce-scatter.3.cloned.1.call-start = ((), (), s32[]{:S(2)}) async-start(), calls=%async_computation.3 | async-start | bytes 2359296 | tf_op jit(solution)/shard_map/reduce_scatter | solution.py:84
  9.0 7.7 %collective-permute-start.1 = (f32[64,1,1,2,512]{4,0,3,2,1:T(8,128)S(1)}, f32[64,1,1,2,512]{4,0,3,2,1:T(8,128)S(1)}, u32[]{:S(2)}, u32[]{:S(2)}) collective-permute-start(f32[64,1,1,2,512]{4,0,3,2,1:T(8,128)S(1)} %get-tuple-element.6), channel_id=1, source_target_pairs={{0,32},{32,64},{64,96},{96,128},{128,160},{160,192},{192,224},{1,3... | collective-permute-start | bytes 786440 | tf_op jit(solution)/shard_map/ppermute | solution.py:18
  10.9 7.5 %collective-permute-start = (f32[64,1,1,2,512]{4,0,3,2,1:T(8,128)S(1)}, f32[64,1,1,2,512]{4,0,3,2,1:T(8,128)S(1)}, u32[]{:S(2)}, u32[]{:S(2)}) collective-permute-start(f32[64,1,1,2,512]{4,0,3,2,1:T(8,128)S(1)} %get-tuple-element.6), channel_id=1, source_target_pairs={{32,0},{64,32},{96,64},{128,96},{160,128},{192,160},{224,192},{33,... | collective-permute-start | bytes 786440 | tf_op jit(solution)/shard_map/ppermute | solution.py:20
  18.5 35.5 %collective-permute-start.2 = (f32[64,3,1,2,512]{4,0,3,2,1:T(8,128)S(1)}, f32[64,3,1,2,512]{4,0,3,2,1:T(8,128)}, u32[]{:S(2)}, u32[]{:S(2)}) collective-permute-start(f32[64,3,1,2,512]{4,0,3,2,1:T(8,128)S(1)} %pad_maximum_fusion), channel_id=1, source_target_pairs={{8,0},{16,8},{24,16},{9,1},{17,9},{25,17},{10,2},{18,10},{26,18},{... | collective-permute-start | bytes 2359304 | tf_op jit(solution)/shard_map/ppermute | solution.py:20
  23.4 34.0 %collective-permute-start.3 = (f32[64,3,1,2,512]{4,0,3,2,1:T(8,128)S(1)}, f32[64,3,1,2,512]{4,0,3,2,1:T(8,128)S(1)}, u32[]{:S(2)}, u32[]{:S(2)}) collective-permute-start(f32[64,3,1,2,512]{4,0,3,2,1:T(8,128)S(1)} %pad_maximum_fusion), channel_id=1, source_target_pairs={{0,8},{8,16},{16,24},{1,9},{9,17},{17,25},{2,10},{10,18},{18,26},{... | collective-permute-start | bytes 2359304 | tf_op jit(solution)/shard_map/ppermute | solution.py:18
  57.4 1.1 copy-start
  149.6 0.7 copy-start.2
  149.6 229.1 %reduce-scatter.5.cloned.1.call-start = ((), (), s32[]{:S(2)}) async-start(), calls=%async_computation.4 | async-start | bytes 2359296 | tf_op jit(solution)/shard_map/reduce_scatter | solution.py:84
  245.7 7.7 %collective-permute-start.5 = (f32[64,1,1,2,512]{4,0,3,2,1:T(8,128)S(1)}, f32[64,1,1,2,512]{4,0,3,2,1:T(8,128)S(1)}, u32[]{:S(2)}, u32[]{:S(2)}) collective-permute-start(f32[64,1,1,2,512]{4,0,3,2,1:T(8,128)S(1)} %get-tuple-element.26), channel_id=1, source_target_pairs={{0,32},{32,64},{64,96},{96,128},{128,160},{160,192},{192,224},{1,3... | collective-permute-start | bytes 786440 | tf_op jit(solution)/shard_map/ppermute | solution.py:18
  247.6 7.5 %collective-permute-start.4 = (f32[64,1,1,2,512]{4,0,3,2,1:T(8,128)S(1)}, f32[64,1,1,2,512]{4,0,3,2,1:T(8,128)S(1)}, u32[]{:S(2)}, u32[]{:S(2)}) collective-permute-start(f32[64,1,1,2,512]{4,0,3,2,1:T(8,128)S(1)} %get-tuple-element.26), channel_id=1, source_target_pairs={{32,0},{64,32},{96,64},{128,96},{160,128},{192,160},{224,192},{33,... | collective-permute-start | bytes 786440 | tf_op jit(solution)/shard_map/ppermute | solution.py:20
  255.2 21.5 %collective-permute-start.6 = (f32[64,3,1,2,512]{4,0,3,2,1:T(8,128)S(1)}, f32[64,3,1,2,512]{4,0,3,2,1:T(8,128)S(1)}, u32[]{:S(2)}, u32[]{:S(2)}) collective-permute-start(f32[64,3,1,2,512]{4,0,3,2,1:T(8,128)S(1)} %pad_maximum_fusion.1), channel_id=1, source_target_pairs={{8,0},{16,8},{24,16},{9,1},{17,9},{25,17},{10,2},{18,10},{26,18},{... | collective-permute-start | bytes 2359304 | tf_op jit(solution)/shard_map/ppermute | solution.py:20
  256.5 22.0 %collective-permute-start.7 = (f32[64,3,1,2,512]{4,0,3,2,1:T(8,128)S(1)}, f32[64,3,1,2,512]{4,0,3,2,1:T(8,128)S(1)}, u32[]{:S(2)}, u32[]{:S(2)}) collective-permute-start(f32[64,3,1,2,512]{4,0,3,2,1:T(8,128)S(1)} %pad_maximum_fusion.1), channel_id=1, source_target_pairs={{0,8},{8,16},{16,24},{1,9},{9,17},{17,25},{2,10},{10,18},{18,26},{... | collective-permute-start | bytes 2359304 | tf_op jit(solution)/shard_map/ppermute | solution.py:18
Sparse Core Ops, SparseCore 0:
  10.0 133.1 all-gather.1
  149.8 90.3 reduce-scatter.2
  285.5 93.2 reduce-scatter.4
where the time goes:
time: 392 us
  waiting for transfers between devices  318 us (81%)
  matrix products  23.9 us (6%)
  starting transfers between devices  23.2 us (6%)
  between operations  17.8 us (5%)
  local copies, waits for them, and re-layouts  5.2 us (1%)
    reduce_scatter x2, waiting for transfers between devices, derivative(): lax.psum_scatter(jnp.einsum('kic,cabkpm->iabpm', op_slice, left_ops, prec...  181 us
    all_gather x1, waiting for transfers between devices, shards(): full_ops = lax.all_gather(operators, 'rows', axis=1, tiled=True)  82.9 us
    ppermute x4, waiting for transfers between devices, padded(): lax.ppermute(head, axis, [((i + 1) % count, i) for i in range(ends)])  44.8 us
    ppermute x4, starting transfers between devices, padded(): lax.ppermute(tail, axis, [(i, (i + 1) % count) for i in range(ends)])  13.2 us
    dot_general x2, matrix products, derivative(): jnp.einsum('kic,cabkpm->iabpm', op_slice, left_ops, precision=PRECISE)  12.8 us
    dot_general x2, matrix products, derivative(): jnp.einsum('iabkpc,kcm->iabpm', right_ops, full_ops, precision=PRECISE)  11.1 us
    ppermute x4, starting transfers between devices, padded(): lax.ppermute(head, axis, [((i + 1) % count, i) for i in range(ends)])  9.87 us
    ppermute x4, waiting for transfers between devices, padded(): lax.ppermute(tail, axis, [(i, (i + 1) % count) for i in range(ends)])  8.42 us
  transfers between devices with their start and end apart: 11, of which 11 were waited for; matrix products, arithmetic and copies ran while one was open for 1% of the time, Pallas kernels for 0%

commit v1 on v0

--- a/solution.py
+++ b/solution.py
@@ -66,7 +66,9 @@
     row_count = density.shape[0]
     count_a = density.shape[1]
     count_b = density.shape[2]
-    full_ops = lax.all_gather(operators, "rows", axis=1, tiled=True)
+    full_ops = jnp.concatenate(
+        lax.all_to_all(jnp.stack([operators] * lax.axis_size("rows")), "rows", 0, 0), axis=1
+    )
     occ_a = (lax.axis_index("occa") * count_a + jnp.arange(count_a)).astype(jnp.float32)[:, None]
     occ_b = (lax.axis_index("occb") * count_b + jnp.arange(count_b)).astype(jnp.float32)[None, :]
     row_start = lax.axis_index("rows") * row_count

time: 392 us -> 417 us (1.064)
  starting transfers between devices: 23.2 us -> 34.4 us
  local copies, waits for them, and re-layouts: 5.2 us -> 14.7 us
  waiting for transfers between devices: 318 us -> 324 us
    ppermute x4, waiting for transfers between devices: 44.8 us -> 130 us  [padded(): lax.ppermute(head, axis, [((i + 1) % count, i) for i in range(ends)])]
    all_gather x1 -> x0, waiting for transfers between devices: 82.9 us -> none  [shards(): full_ops = lax.all_gather(operators, 'rows', axis=1, tiled=True)]
    all_to_all x0 -> x1, starting transfers between devices: none -> 11.2 us  [shards(): lax.all_to_all(jnp.stack([operators] * lax.axis_size('rows')), 'rows', 0, 0)]
    reduce_scatter x2, waiting for transfers between devices: 181 us -> 188 us  [derivative(): lax.psum_scatter(jnp.einsum('kic,cabkpm->iabpm', op_slice, left_ops, prec...]
  transfers between devices with their start and end apart: 11 -> 11, of which waited for: 11 -> 9; matrix products, arithmetic and copies ran while one was open for 1% -> 1% of each run, Pallas kernels for 0% -> 0%
where the time goes in v1:
time: 417 us
  waiting for transfers between devices  324 us (78%)
  starting transfers between devices  34.4 us (8%)
  matrix products  22.6 us (5%)
  between operations  18.4 us (4%)
  local copies, waits for them, and re-layouts  14.7 us (4%)
    reduce_scatter x2, waiting for transfers between devices, derivative(): lax.psum_scatter(jnp.einsum('kic,cabkpm->iabpm', op_slice, left_ops, prec...  188 us
    ppermute x4, waiting for transfers between devices, padded(): lax.ppermute(head, axis, [((i + 1) % count, i) for i in range(ends)])  130 us
    ppermute x4, starting transfers between devices, padded(): lax.ppermute(tail, axis, [(i, (i + 1) % count) for i in range(ends)])  13.2 us
    dot_general x2, matrix products, derivative(): jnp.einsum('kic,cabkpm->iabpm', op_slice, left_ops, precision=PRECISE)  11.5 us
    all_to_all x1, starting transfers between devices, shards(): lax.all_to_all(jnp.stack([operators] * lax.axis_size('rows')), 'rows', 0, 0)  11.2 us
    dot_general x2, matrix products, derivative(): jnp.einsum('iabkpc,kcm->iabpm', right_ops, full_ops, precision=PRECISE)  11.1 us
    ppermute x4, starting transfers between devices, padded(): lax.ppermute(head, axis, [((i + 1) % count, i) for i in range(ends)])  9.87 us
  transfers between devices with their start and end apart: 11, of which 9 were waited for; matrix products, arithmetic and copies ran while one was open for 1% of the time, Pallas kernels for 0%

profile of v1, /device:TPU:2, one launch (start us, length us, event | category | flops | bytes accessed | tf_op | source)
XLA Modules:
  0.0 416.8 jit_solution(2988087051463981139)
XLA Ops:
  6.5 4.1 stack.97
  10.7 0.0 copy-start.2
  10.7 11.2 %all-to-all-start = ((f32[8,5,64,512]{3,2,1,0:T(8,128)}), f32[8,5,64,512]{3,2,1,0:T(8,128)}, u32[]{:S(2)}, u32[]{:S(2)}) async-start(f32[8,5,64,512]{3,2,1,0:T(8,128)} %stack.97), calls=%async_computation | async-start | bytes 10485760 | tf_op jit(solution)/shard_map/all_to_all | solution.py:70
  21.9 0.0 copy-start.3
  21.9 0.0 reduce-scatter.3.cloned.1.call-start
  22.6 0.0 copy-done.2
  22.6 0.1 bitcast_dynamic-update-slice_fusion.5
  22.7 1.9 collective-permute-start.1
  24.6 3.6 collective-permute-start
  28.3 2.1 collective-permute-done.1
  30.4 1.8 collective-permute-done
  32.1 0.1 pad_maximum_fusion
  32.2 1.3 collective-permute-start.2
  33.7 0.0 copy-done.3
  33.7 0.7 fusion.37
  36.9 0.1 stack.115
  37.0 0.1 stack.111
  37.1 4.6 %collective-permute-start.3 = (f32[64,3,1,2,512]{4,0,3,2,1:T(8,128)S(1)}, f32[64,3,1,2,512]{4,0,3,2,1:T(8,128)S(1)}, u32[]{:S(2)}, u32[]{:S(2)}) collective-permute-start(f32[64,3,1,2,512]{4,0,3,2,1:T(8,128)S(1)} %pad_maximum_fusion), channel_id=1, source_target_pairs={{0,8},{8,16},{16,24},{1,9},{9,17},{17,25},{2,10},{10,18},{18,26},{... | collective-permute-start | bytes 2359304 | tf_op jit(solution)/shard_map/ppermute | solution.py:18
  41.7 0.1 fusion.30
  41.8 111.2 %collective-permute-done.2 = f32[64,3,1,2,512]{4,0,3,2,1:T(8,128)} collective-permute-done((f32[64,3,1,2,512]{4,0,3,2,1:T(8,128)S(1)}, f32[64,3,1,2,512]{4,0,3,2,1:T(8,128)}, u32[]{:S(2)}, u32[]{:S(2)}) %collective-permute-start.2) | collective-permute-done | bytes 786464 | tf_op jit(solution)/shard_map/ppermute | solution.py:20
  153.0 1.0 fusion.27
  154.0 0.0 collective-permute-done.3
  154.0 0.0 copy-start.1
  154.0 1.1 copy-done.1
  155.1 1.8 multiply_subtract_fusion.2
  156.8 0.0 all-to-all-done
  156.8 3.1 copy.27
  159.9 0.0 copy-start
  159.9 2.3 copy-done
  162.3 5.1 %convolution_bitcast_fusion.1 = f32[512,1,1,2,512]{4,0,3,2,1:T(8,128)} fusion(f32[64,1,1,5,1,512]{5,0,3,4,2,1:T(8,128)S(1)} %get-tuple-element.17, f32[64,1,1,5,1,512]{5,0,3,4,2,1:T(8,128)S(1)} %get-tuple-element.18, f32[5,512,512]{2,1,0:T(8,128)S(1)} %bitcast.165, s32[]{:T(128)S(6)} %select_n.4), kind=kOutput, calls=%fused_computation.1 | convolution fusion | flops 2013593600 | bytes 4718596 | tf_op jit(solution)/shard_map/kic,cabkpm->iabpm/dot_general | solution.py:87
  167.3 0.0 copy-start.4
  167.3 0.0 reduce-scatter.3.cloned.1.call-update
  167.4 0.0 reduce-scatter.5.cloned.1.call-start
  167.4 0.6 copy-done.4
  168.0 0.7 fusion.38
  170.0 94.9 %reduce-scatter.3.cloned.1.call-done = f32[64,1,1,2,512]{4,0,3,2,1:T(8,128)} async-done(((f32[512,1,1,2,512]{4,0,3,2,1:T(8,128)}), f32[64,1,1,2,512]{4,0,3,2,1:T(8,128)}) %reduce-scatter.3.cloned.1.call-update) | async-done | bytes 262160 | tf_op jit(solution)/shard_map/reduce_scatter | solution.py:86
  264.9 5.5 %bitcast_dynamic-update-slice_fusion.2 = (f32[64,1,1,5,2,512]{5,0,3,4,2,1:T(8,128)S(1)}, f32[64,1,1,2,512]{4,0,3,2,1:T(8,128)S(1)}) fusion(f32[]{:T(128)} %bitcast, f32[64,1,1,2,512]{4,0,3,2,1:T(8,128)S(1)} %get-tuple-element.6, f32[]{:T(128)} %bitcast.33, f32[64,1,1,2,512]{4,0,3,2,1:T(8,128)} %reduce-scatter.3.cloned.1.call-done, ...), kind=kOutput, calls=%fused_computation.52 | convolution fusion | flops 2013855744 | bytes 7602184 | tf_op jit(solution)/shard_map/iabkpc,kcm->iabpm/dot_general | solution.py:83
  270.4 1.9 collective-permute-start.5
  272.4 3.6 collective-permute-start.4
  276.0 2.1 collective-permute-done.5
  278.1 1.8 collective-permute-done.4
  279.9 0.1 pad_maximum_fusion.1
  280.0 1.3 collective-permute-start.6
  281.3 4.8 %collective-permute-start.7 = (f32[64,3,1,2,512]{4,0,3,2,1:T(8,128)S(1)}, f32[64,3,1,2,512]{4,0,3,2,1:T(8,128)S(1)}, u32[]{:S(2)}, u32[]{:S(2)}) collective-permute-start(f32[64,3,1,2,512]{4,0,3,2,1:T(8,128)S(1)} %pad_maximum_fusion.1), channel_id=1, source_target_pairs={{0,8},{8,16},{16,24},{1,9},{9,17},{17,25},{2,10},{10,18},{18,26},{... | collective-permute-start | bytes 2359304 | tf_op jit(solution)/shard_map/ppermute | solution.py:18
  286.1 15.4 %collective-permute-done.6 = f32[64,3,1,2,512]{4,0,3,2,1:T(8,128)S(1)} collective-permute-done((f32[64,3,1,2,512]{4,0,3,2,1:T(8,128)S(1)}, f32[64,3,1,2,512]{4,0,3,2,1:T(8,128)S(1)}, u32[]{:S(2)}, u32[]{:S(2)}) %collective-permute-start.6) | collective-permute-done | bytes 786464 | tf_op jit(solution)/shard_map/ppermute | solution.py:20
  301.6 1.8 collective-permute-done.7
  303.3 0.3 multiply_subtract_fusion
  303.7 6.4 %convolution_bitcast_fusion = f32[512,1,1,2,512]{4,0,3,2,1:T(8,128)} fusion(f32[64,1,1,5,1,512]{5,0,3,4,2,1:T(8,128)S(1)} %get-tuple-element.15, f32[64,1,1,5,1,512]{5,0,3,4,2,1:T(8,128)S(1)} %get-tuple-element.16, f32[5,512,512]{2,1,0:T(8,128)} %bitcast.167, s32[]{:T(128)S(6)} %select_n.4), kind=kOutput, calls=%fused_computation | convolution fusion | flops 2013593600 | bytes 4718596 | tf_op jit(solution)/shard_map/kic,cabkpm->iabpm/dot_general | solution.py:87
  310.1 0.0 reduce-scatter.5.cloned.1.call-update
  310.1 93.4 %reduce-scatter.5.cloned.1.call-done = f32[64,1,1,2,512]{4,0,3,2,1:T(8,128)} async-done(((f32[512,1,1,2,512]{4,0,3,2,1:T(8,128)}), f32[64,1,1,2,512]{4,0,3,2,1:T(8,128)}) %reduce-scatter.5.cloned.1.call-update) | async-done | bytes 262160 | tf_op jit(solution)/shard_map/reduce_scatter | solution.py:86
  403.5 5.6 %fusion.23 = f32[64,1,1,2,512]{4,0,3,2,1:T(8,128)S(1)} fusion(f32[64,1,1,2,512]{4,0,3,2,1:T(8,128)} %reduce-scatter.5.cloned.1.call-done, f32[5,512,512,1]{2,1,0,3:T(8,128)} %bitcast.168, f32[64,1,1,5,1,512]{5,0,3,4,2,1:T(8,128)S(1)} %get-tuple-element.8, f32[64,1,1,5,1,512]{5,0,3,4,2,1:T(8,128)S(1)} %get-tuple-element.7, ...), kind=kOutput, calls=%fused_computation.29 | convolution fusion | flops 2014117888 | bytes 7602184 | tf_op jit(solution)/shard_map/iabkpc,kcm->iabpm/dot_general | solution.py:83
  409.1 0.9 copy.35
  (9 shorter events, 0.1 us)
Async XLA Ops:
  10.7 11.9 %copy-start.2 = (f32[64,1,1,2,512]{4,3,2,1,0:T(2,128)S(1)}, f32[64,1,1,2,512]{4,3,2,1,0:T(2,128)}, u32[]{:S(2)}) copy-start(f32[64,1,1,2,512]{4,3,2,1,0:T(2,128)} %param.5) | copy-start | bytes 786436
  10.7 146.2 %all-to-all-start = ((f32[8,5,64,512]{3,2,1,0:T(8,128)}), f32[8,5,64,512]{3,2,1,0:T(8,128)}, u32[]{:S(2)}, u32[]{:S(2)}) async-start(f32[8,5,64,512]{3,2,1,0:T(8,128)} %stack.97), calls=%async_computation | async-start | bytes 10485760 | tf_op jit(solution)/shard_map/all_to_all | solution.py:70
  21.9 11.8 %copy-start.3 = (f32[2,2]{1,0:T(2,128)S(1)}, f32[2,2]{1,0:T(2,128)}, u32[]{:S(2)}) copy-start(f32[2,2]{1,0:T(2,128)} %param.8) | copy-start | bytes 52
  21.9 243.0 %reduce-scatter.3.cloned.1.call-start = ((), (), s32[]{:S(2)}) async-start(), calls=%async_computation.3 | async-start | bytes 2359296 | tf_op jit(solution)/shard_map/reduce_scatter | solution.py:86
  22.7 7.7 %collective-permute-start.1 = (f32[64,1,1,2,512]{4,0,3,2,1:T(8,128)S(1)}, f32[64,1,1,2,512]{4,0,3,2,1:T(8,128)S(1)}, u32[]{:S(2)}, u32[]{:S(2)}) collective-permute-start(f32[64,1,1,2,512]{4,0,3,2,1:T(8,128)S(1)} %get-tuple-element.6), channel_id=1, source_target_pairs={{0,32},{32,64},{64,96},{96,128},{128,160},{160,192},{192,224},{1,3... | collective-permute-start | bytes 786440 | tf_op jit(solution)/shard_map/ppermute | solution.py:18
  24.6 7.5 %collective-permute-start = (f32[64,1,1,2,512]{4,0,3,2,1:T(8,128)S(1)}, f32[64,1,1,2,512]{4,0,3,2,1:T(8,128)S(1)}, u32[]{:S(2)}, u32[]{:S(2)}) collective-permute-start(f32[64,1,1,2,512]{4,0,3,2,1:T(8,128)S(1)} %get-tuple-element.6), channel_id=1, source_target_pairs={{32,0},{64,32},{96,64},{128,96},{160,128},{192,160},{224,192},{33,... | collective-permute-start | bytes 786440 | tf_op jit(solution)/shard_map/ppermute | solution.py:20
  32.2 120.8 %collective-permute-start.2 = (f32[64,3,1,2,512]{4,0,3,2,1:T(8,128)S(1)}, f32[64,3,1,2,512]{4,0,3,2,1:T(8,128)}, u32[]{:S(2)}, u32[]{:S(2)}) collective-permute-start(f32[64,3,1,2,512]{4,0,3,2,1:T(8,128)S(1)} %pad_maximum_fusion), channel_id=1, source_target_pairs={{8,0},{16,8},{24,16},{9,1},{17,9},{25,17},{10,2},{18,10},{26,18},{... | collective-permute-start | bytes 2359304 | tf_op jit(solution)/shard_map/ppermute | solution.py:20
  37.1 116.9 %collective-permute-start.3 = (f32[64,3,1,2,512]{4,0,3,2,1:T(8,128)S(1)}, f32[64,3,1,2,512]{4,0,3,2,1:T(8,128)S(1)}, u32[]{:S(2)}, u32[]{:S(2)}) collective-permute-start(f32[64,3,1,2,512]{4,0,3,2,1:T(8,128)S(1)} %pad_maximum_fusion), channel_id=1, source_target_pairs={{0,8},{8,16},{16,24},{1,9},{9,17},{17,25},{2,10},{10,18},{18,26},{... | collective-permute-start | bytes 2359304 | tf_op jit(solution)/shard_map/ppermute | solution.py:18
  154.0 1.1 copy-start.1
  159.9 2.3 copy-start
  167.3 0.7 copy-start.4
  167.4 236.2 %reduce-scatter.5.cloned.1.call-start = ((), (), s32[]{:S(2)}) async-start(), calls=%async_computation.4 | async-start | bytes 2359296 | tf_op jit(solution)/shard_map/reduce_scatter | solution.py:86
  270.4 7.7 %collective-permute-start.5 = (f32[64,1,1,2,512]{4,0,3,2,1:T(8,128)S(1)}, f32[64,1,1,2,512]{4,0,3,2,1:T(8,128)S(1)}, u32[]{:S(2)}, u32[]{:S(2)}) collective-permute-start(f32[64,1,1,2,512]{4,0,3,2,1:T(8,128)S(1)} %get-tuple-element.26), channel_id=1, source_target_pairs={{0,32},{32,64},{64,96},{96,128},{128,160},{160,192},{192,224},{1,3... | collective-permute-start | bytes 786440 | tf_op jit(solution)/shard_map/ppermute | solution.py:18
  272.4 7.5 %collective-permute-start.4 = (f32[64,1,1,2,512]{4,0,3,2,1:T(8,128)S(1)}, f32[64,1,1,2,512]{4,0,3,2,1:T(8,128)S(1)}, u32[]{:S(2)}, u32[]{:S(2)}) collective-permute-start(f32[64,1,1,2,512]{4,0,3,2,1:T(8,128)S(1)} %get-tuple-element.26), channel_id=1, source_target_pairs={{32,0},{64,32},{96,64},{128,96},{160,128},{192,160},{224,192},{33,... | collective-permute-start | bytes 786440 | tf_op jit(solution)/shard_map/ppermute | solution.py:20
  280.0 21.6 %collective-permute-start.6 = (f32[64,3,1,2,512]{4,0,3,2,1:T(8,128)S(1)}, f32[64,3,1,2,512]{4,0,3,2,1:T(8,128)S(1)}, u32[]{:S(2)}, u32[]{:S(2)}) collective-permute-start(f32[64,3,1,2,512]{4,0,3,2,1:T(8,128)S(1)} %pad_maximum_fusion.1), channel_id=1, source_target_pairs={{8,0},{16,8},{24,16},{9,1},{17,9},{25,17},{10,2},{18,10},{26,18},{... | collective-permute-start | bytes 2359304 | tf_op jit(solution)/shard_map/ppermute | solution.py:20
  281.3 22.0 %collective-permute-start.7 = (f32[64,3,1,2,512]{4,0,3,2,1:T(8,128)S(1)}, f32[64,3,1,2,512]{4,0,3,2,1:T(8,128)S(1)}, u32[]{:S(2)}, u32[]{:S(2)}) collective-permute-start(f32[64,3,1,2,512]{4,0,3,2,1:T(8,128)S(1)} %pad_maximum_fusion.1), channel_id=1, source_target_pairs={{0,8},{8,16},{16,24},{1,9},{9,17},{17,25},{2,10},{10,18},{18,26},{... | collective-permute-start | bytes 2359304 | tf_op jit(solution)/shard_map/ppermute | solution.py:18
Sparse Core Ops, SparseCore 0:
  167.5 97.3 reduce-scatter.2
  310.2 93.2 reduce-scatter.4
